TPU v7x, 128 devices: a whole 4x4x4 slice. The times are simulated.
128 devices in a mesh: heads: 2 (over z_hi), slab: 64 (over z_lo, y, x, core).
Axes of the slice: x: 4, y: 4, z: 4 (z_hi: 2, z_lo: 2; z = z_hi * 2 + z_lo), core: 2. Of those that a mesh axis runs over, the one named last changes fastest.
Arguments:
- tokens: bfloat16 [64, 384, 3072], P('slab', 'heads'), may hold values from -400 to 400
- qkv_weight: bfloat16 [3072, 4608], P(None, 'heads'), may hold values from -1 to 1
- out_weight: bfloat16 [1536, 3072], P('heads'), may hold values from -0.15625 to 0.15625
- query_gain: float32 [128], replicated, may hold values from 0.6 to 4.5
- key_gain: float32 [128], replicated, may hold values from 0.6 to 4.5
- mod_shift: float32 [3072], replicated, may hold values from -3 to 3
- mod_scale: float32 [3072], replicated, may hold values from -0.5 to 1.5
- branch_gate: float32 [3072], replicated, may hold values from 1 to 3
- block_mask: int32 [64, 27], P('slab'), may hold values 0 or 1
Outputs:
- attended: bfloat16 [64, 384, 3072], P('slab', 'heads')
All inputs are finite; a program needn't handle non-finite values. No bound on the sum of `block_mask` on one device may be relied on, other than what follows from the above.
Results may differ from a plain program's by a relative error of at most 0.0095.
The roundings to bfloat16 on the way count: a program that leaves them out, or rounds other values in their place, can miss the bound.
Values may be sent and summed in bfloat16 or wider, within the bound.
No kernel may reach another device: no remote copies, remote signals or barrier semaphores. Data moves between devices by JAX's collectives and lax.ppermute only.
A program may use at most 320 MiB of HBM per device.

v0:
```python
import jax
import jax.numpy as jnp
from jax import lax
from jax.sharding import PartitionSpec as P

GT = 4


def shifted(value, axis, steps):
    count = lax.axis_size(axis)
    leading, last = (max(0, -steps), min(count, count - steps))
    return lax.ppermute(value, axis, [(source, source + steps) for source in range(leading, last)])


def modulate(token_rows, mod_shift, mod_scale):
    token_rows = token_rows.astype(jnp.float32)
    row_mean = jnp.mean(token_rows, axis=-1, keepdims=True)
    centered = token_rows - row_mean
    variance = jnp.mean(centered * centered, axis=-1, keepdims=True)
    return (centered * lax.rsqrt(variance + 1e-06) * (1.0 + mod_scale) + mod_shift).astype(
        jnp.bfloat16
    )


def head_norm(head_rows, scale_gain):
    head_rows = head_rows.astype(jnp.float32)
    return (
        head_rows
        * lax.rsqrt(jnp.mean(head_rows * head_rows, axis=-1, keepdims=True) + 1e-06)
        * scale_gain
    )


def window_live(mask_row, slab_at, grid_t, grid_h, grid_w):
    time_at = slab_at // (grid_h * grid_w)
    height_at = slab_at // grid_w % grid_h
    width_at = slab_at % grid_w
    offsets = jnp.arange(27, dtype=jnp.int32)
    step_t = offsets // 9 - 1
    step_h = offsets // 3 % 3 - 1
    step_w = offsets % 3 - 1
    inside = (time_at + step_t >= 0) & (time_at + step_t < grid_t)
    inside = inside & (height_at + step_h >= 0) & (height_at + step_h < grid_h)
    inside = inside & (width_at + step_w >= 0) & (width_at + step_w < grid_w)
    return inside & ((offsets == 13) | (mask_row == 1))


def soft_weights(scores, live):
    keep = live[None, :, None]
    masked = jnp.where(keep, scores, -1e30)
    row_top = jnp.max(masked, axis=(1, 2), keepdims=True)
    raised = jnp.where(keep, jnp.exp(masked - row_top), 0.0)
    return (raised / jnp.sum(raised, axis=(1, 2), keepdims=True)).astype(jnp.bfloat16)


def collect_window(packed, grid_h, grid_w):
    plane = grid_h * grid_w
    blocks = []
    for order_at in range(27):
        if order_at == 13:
            blocks.append(packed)
        else:
            offset = (
                (order_at // 9 - 1) * plane + (order_at // 3 % 3 - 1) * grid_w + (order_at % 3 - 1)
            )
            blocks.append(shifted(packed, "slab", -offset))
    return jnp.concatenate(blocks, axis=0)


def on_device(
    tokens,
    qkv_weight,
    out_weight,
    query_gain,
    key_gain,
    mod_shift,
    mod_scale,
    branch_gate,
    block_mask,
):
    head_dim = query_gain.shape[0]
    group_width = out_weight.shape[0]
    group_heads = group_width // head_dim
    normed = modulate(tokens[0], mod_shift, mod_scale)
    projected = jnp.dot(
        lax.all_gather(normed, "heads", axis=0, tiled=True),
        qkv_weight,
        preferred_element_type=jnp.float32,
    ).astype(jnp.bfloat16)
    tile_tok = projected.shape[0]
    pieces = projected.reshape(tile_tok, group_heads, 3, head_dim)
    queries = (head_norm(pieces[:, :, 0], query_gain) * head_dim ** (-0.5)).astype(jnp.bfloat16)
    own_keys = head_norm(pieces[:, :, 1], key_gain).astype(jnp.bfloat16)
    packed = jnp.concatenate(
        [own_keys.reshape(tile_tok, group_width), pieces[:, :, 2].reshape(tile_tok, group_width)],
        axis=1,
    )[None]
    slab_count = lax.axis_size("slab")
    slab_at = lax.axis_index("slab")
    grid_h = min(4, slab_count // 8)
    grid_w = slab_count // (GT * grid_h)
    window = collect_window(packed, grid_h, grid_w)
    window_keys = window[:, :, :group_width].reshape(27, tile_tok, group_heads, head_dim)
    window_values = window[:, :, group_width:].reshape(27, tile_tok, group_heads, head_dim)
    live = window_live(block_mask[0], slab_at, GT, grid_h, grid_w)

    def one_head(head_at):
        query_rows = lax.dynamic_index_in_dim(queries, head_at, 1, keepdims=False)
        key_rows = lax.dynamic_index_in_dim(window_keys, head_at, 2, keepdims=False)
        value_rows = lax.dynamic_index_in_dim(window_values, head_at, 2, keepdims=False)
        scores = jnp.einsum("qd,okd->qok", query_rows, key_rows, preferred_element_type=jnp.float32)
        weights = soft_weights(scores, live)
        return jnp.einsum(
            "qok,okd->qd", weights, value_rows, preferred_element_type=jnp.float32
        ).astype(jnp.bfloat16)

    per_head = lax.map(one_head, jnp.arange(group_heads, dtype=jnp.int32))
    attention = jnp.transpose(per_head, (1, 0, 2)).reshape(tile_tok, group_width)
    summed = lax.psum_scatter(
        jnp.dot(attention, out_weight, preferred_element_type=jnp.float32).astype(jnp.bfloat16),
        "heads",
        scatter_dimension=0,
        tiled=True,
    ).astype(jnp.float32)
    return (branch_gate * summed).astype(jnp.bfloat16)[None]


def solution(mesh):
    in_specs = (
        P("slab", "heads", None),
        P(None, "heads"),
        P("heads", None),
        P(),
        P(),
        P(),
        P(),
        P(),
        P("slab", None),
    )
    out_specs = P("slab", "heads", None)
    return jax.shard_map(
        on_device, mesh=mesh, in_specs=in_specs, out_specs=out_specs, check_vma=False
    )
```

profile of v0, /device:TPU:1, one launch (start us, length us, event | category | flops | bytes accessed | tf_op | source)
XLA Modules:
  0.0 1011.1 jit_solution(6357708120327719233)
XLA Ops:
  7.3 1.5 convert_reduce_fusion
  8.8 1.7 fusion.25
  10.5 2.8 fusion.28
  13.4 43.4 %all-gather.2.cloned.1.call-done = bf16[384,3072]{1,0:T(8,128)(2,1)} async-done(((bf16[192,3072]{1,0:T(8,128)(2,1)}), bf16[384,3072]{1,0:T(8,128)(2,1)}) %all-gather.2.cloned.1.call-update) | async-done | bytes 2359312 | tf_op jit(solution)/shard_map/all_gather | solution.py:86
  56.8 11.2 %convolution_convert_fusion.1 = bf16[384,2304]{1,0:T(8,128)(2,1)S(1)} fusion(bf16[384,3072]{1,0:T(8,128)(2,1)} %all-gather.2.cloned.1.call-done, bf16[3072,2304]{1,0:T(8,128)(2,1)} %param.12), kind=kOutput, calls=%fused_computation.21 | convolution fusion | flops 5436702720 | bytes 18284544 | tf_op jit(solution)/shard_map/dot_general | solution.py:85
  70.8 8.5 collective-permute-start
  79.3 2.5 collective-permute-start.1
  81.9 6.1 collective-permute-start.2
  88.0 1.4 collective-permute-start.3
  89.4 1.4 collective-permute-start.4
  91.1 7.6 collective-permute-done
  98.7 24.0 %collective-permute-start.5 = (bf16[1,384,1536]{1,2,0:T(8,128)(2,1)}, bf16[1,384,1536]{1,2,0:T(8,128)(2,1)S(1)}, u32[]{:S(2)}, u32[]{:S(2)}) collective-permute-start(bf16[1,384,1536]{1,2,0:T(8,128)(2,1)} %maximum_bitcast_fusion), channel_id=1, source_target_pairs={{0,15},{1,16},{2,17},{3,18},{4,19},{5,20},{6,21},{7,22},{8,23},{9,... | collective-permute-start | bytes 3538952 | tf_op jit(solution)/shard_map/ppermute | solution.py:12
  122.7 1.4 constant_dynamic-update-slice_fusion.27
  124.2 47.3 %collective-permute-start.6 = (bf16[1,384,1536]{1,2,0:T(8,128)(2,1)}, bf16[1,384,1536]{1,2,0:T(8,128)(2,1)S(1)}, u32[]{:S(2)}, u32[]{:S(2)}) collective-permute-start(bf16[1,384,1536]{1,2,0:T(8,128)(2,1)} %maximum_bitcast_fusion), channel_id=1, source_target_pairs={{0,13},{1,14},{2,15},{3,16},{4,17},{5,18},{6,19},{7,20},{8,21},{9,... | collective-permute-start | bytes 3538952 | tf_op jit(solution)/shard_map/ppermute | solution.py:12
  171.5 1.5 constant_dynamic-update-slice_fusion.26
  173.0 21.9 %collective-permute-start.7 = (bf16[1,384,1536]{1,2,0:T(8,128)(2,1)}, bf16[1,384,1536]{1,2,0:T(8,128)(2,1)S(1)}, u32[]{:S(2)}, u32[]{:S(2)}) collective-permute-start(bf16[1,384,1536]{1,2,0:T(8,128)(2,1)} %maximum_bitcast_fusion), channel_id=1, source_target_pairs={{0,12},{1,13},{2,14},{3,15},{4,16},{5,17},{6,18},{7,19},{8,20},{9,... | collective-permute-start | bytes 3538952 | tf_op jit(solution)/shard_map/ppermute | solution.py:12
  194.9 1.5 constant_dynamic-update-slice_fusion.25
  196.4 39.4 %collective-permute-start.8 = (bf16[1,384,1536]{1,2,0:T(8,128)(2,1)}, bf16[1,384,1536]{1,2,0:T(8,128)(2,1)S(1)}, u32[]{:S(2)}, u32[]{:S(2)}) collective-permute-start(bf16[1,384,1536]{1,2,0:T(8,128)(2,1)} %maximum_bitcast_fusion), channel_id=1, source_target_pairs={{0,11},{1,12},{2,13},{3,14},{4,15},{5,16},{6,17},{7,18},{8,19},{9,... | collective-permute-start | bytes 3538952 | tf_op jit(solution)/shard_map/ppermute | solution.py:12
  236.1 100.3 %collective-permute-start.9 = (bf16[1,384,1536]{1,2,0:T(8,128)(2,1)}, bf16[1,384,1536]{1,2,0:T(8,128)(2,1)S(1)}, u32[]{:S(2)}, u32[]{:S(2)}) collective-permute-start(bf16[1,384,1536]{1,2,0:T(8,128)(2,1)} %maximum_bitcast_fusion), channel_id=1, source_target_pairs={{0,5},{1,6},{2,7},{3,8},{4,9},{5,10},{6,11},{7,12},{8,13},{9,14},{... | collective-permute-start | bytes 3538952 | tf_op jit(solution)/shard_map/ppermute | solution.py:12
  336.7 1.4 collective-permute-start.10
  338.3 1.4 collective-permute-start.11
  340.0 3.3 collective-permute-start.12
  343.6 1.9 collective-permute-start.13
  345.7 31.7 %collective-permute-done.9 = bf16[1,384,1536]{1,2,0:T(8,128)(2,1)S(1)} collective-permute-done((bf16[1,384,1536]{1,2,0:T(8,128)(2,1)}, bf16[1,384,1536]{1,2,0:T(8,128)(2,1)S(1)}, u32[]{:S(2)}, u32[]{:S(2)}) %collective-permute-start.9) | collective-permute-done | bytes 1179680 | tf_op jit(solution)/shard_map/ppermute | solution.py:12
  378.9 1.3 collective-permute-start.15
  380.5 2.9 collective-permute-done.11
  385.0 11.1 %collective-permute-done.12 = bf16[1,384,1536]{1,2,0:T(8,128)(2,1)S(1)} collective-permute-done((bf16[1,384,1536]{1,2,0:T(8,128)(2,1)}, bf16[1,384,1536]{1,2,0:T(8,128)(2,1)S(1)}, u32[]{:S(2)}, u32[]{:S(2)}) %collective-permute-start.12) | collective-permute-done | bytes 1179680 | tf_op jit(solution)/shard_map/ppermute | solution.py:12
  397.8 2.6 collective-permute-done.13
  401.9 39.6 %collective-permute-done.14 = bf16[1,384,1536]{1,2,0:T(8,128)(2,1)S(1)} collective-permute-done((bf16[1,384,1536]{1,2,0:T(8,128)(2,1)}, bf16[1,384,1536]{1,2,0:T(8,128)(2,1)S(1)}, u32[]{:S(2)}, u32[]{:S(2)}) %collective-permute-start.14) | collective-permute-done | bytes 1179680 | tf_op jit(solution)/shard_map/ppermute | solution.py:12
  441.5 1.3 collective-permute-start.19
  443.1 1.5 collective-permute-start.20
  444.8 34.9 %collective-permute-done.16 = bf16[1,384,1536]{1,2,0:T(8,128)(2,1)S(1)} collective-permute-done((bf16[1,384,1536]{1,2,0:T(8,128)(2,1)}, bf16[1,384,1536]{1,2,0:T(8,128)(2,1)S(1)}, u32[]{:S(2)}, u32[]{:S(2)}) %collective-permute-start.16) | collective-permute-done | bytes 1179680 | tf_op jit(solution)/shard_map/ppermute | solution.py:12
  479.6 1.3 collective-permute-start.21
  481.2 7.9 collective-permute-done.17
  489.1 1.3 collective-permute-start.22
  490.6 13.7 %collective-permute-done.18 = bf16[1,384,1536]{1,2,0:T(8,128)(2,1)S(1)} collective-permute-done((bf16[1,384,1536]{1,2,0:T(8,128)(2,1)}, bf16[1,384,1536]{1,2,0:T(8,128)(2,1)S(1)}, u32[]{:S(2)}, u32[]{:S(2)}) %collective-permute-start.18) | collective-permute-done | bytes 1179680 | tf_op jit(solution)/shard_map/ppermute | solution.py:12
  505.8 43.6 %collective-permute-done.19 = bf16[1,384,1536]{1,2,0:T(8,128)(2,1)S(1)} collective-permute-done((bf16[1,384,1536]{1,2,0:T(8,128)(2,1)}, bf16[1,384,1536]{1,2,0:T(8,128)(2,1)S(1)}, u32[]{:S(2)}, u32[]{:S(2)}) %collective-permute-start.19) | collective-permute-done | bytes 1179680 | tf_op jit(solution)/shard_map/ppermute | solution.py:12
  551.0 1.3 collective-permute-start.25
  552.8 4.7 collective-permute-done.22
  557.8 91.0 %collective-permute-done.23 = bf16[1,384,1536]{1,2,0:T(8,128)(2,1)S(1)} collective-permute-done((bf16[1,384,1536]{1,2,0:T(8,128)(2,1)}, bf16[1,384,1536]{1,2,0:T(8,128)(2,1)S(1)}, u32[]{:S(2)}, u32[]{:S(2)}) %collective-permute-start.23) | collective-permute-done | bytes 1179680 | tf_op jit(solution)/shard_map/ppermute | solution.py:12
  649.3 55.4 %collective-permute-done.25 = bf16[1,384,1536]{1,2,0:T(8,128)(2,1)S(1)} collective-permute-done((bf16[1,384,1536]{1,2,0:T(8,128)(2,1)}, bf16[1,384,1536]{1,2,0:T(8,128)(2,1)S(1)}, u32[]{:S(2)}, u32[]{:S(2)}) %collective-permute-start.25) | collective-permute-done | bytes 1179680 | tf_op jit(solution)/shard_map/ppermute | solution.py:12
  704.9 10.8 %fusion.44 = (bf16[27,384,768]{1,2,0:T(8,128)(2,1)}, bf16[27,384,768]{1,2,0:T(8,128)(2,1)}) fusion(bf16[27,384,1536]{1,2,0:T(8,128)(2,1)S(1)} %constant_dynamic-update-slice_fusion.1), kind=kLoop, calls=%fused_computation.97 | loop fusion | bytes 63700992 | tf_op jit(solution)/shard_map/slice | solution.py:104
  715.8 193.5 %while.10 = (s32[]{:T(128)}, bf16[6,384,128]{1,2,0:T(8,128)(2,1)S(1)}, pred[27]{0:T(512)(128)(4,1)S(1)}, s32[6]{0:T(128)S(1)}, bf16[384,6,128]{0,2,1:T(8,128)(2,...) while((s32[]{:T(128)}, ...), condition=%wide.region_7.8_spmd, body=%wide.region_4.7_spmd.sunk | while | flops 2082274560 | bytes 53683416 | solution.py:117
  718.3 9.9 select_reduce_fusion.2
  728.2 9.3 fusion.53
  737.5 10.4 %fusion.54 = bf16[1,384,128]{2,1,0:T(8,128)(2,1)S(1)} fusion(bf16[27,384,6,128]{1,3,2,0:T(8,128)(2,1)} %get-tuple-element.143, s32[]{:T(128)S(6)} %select_n.126, f32[384,27,384]{0,2,1:T(8,128)} %get-tuple-element.115, f32[384]{0:T(512)S(1)} %fusion.53, f32[384]{0:T(512)S(1)} %get-tuple-element.116, pred[27]{0:T(512)(128)(4,1)S(1)} %get-tuple-element.139), kind=kOutput, calls=%fused_computation.12.clone.1 | convolution fusion | flops 1039171584 | bytes 18680864 | tf_op jit(solution)/shard_map/while/body/eval_jaxpr/qok,okd->qd/dot_general | solution.py:113
  750.6 9.9 select_reduce_fusion.2
  760.5 9.3 fusion.53
  769.7 10.4 %fusion.54 = bf16[1,384,128]{2,1,0:T(8,128)(2,1)S(1)} fusion(bf16[27,384,6,128]{1,3,2,0:T(8,128)(2,1)} %get-tuple-element.143, s32[]{:T(128)S(6)} %select_n.126, f32[384,27,384]{0,2,1:T(8,128)} %get-tuple-element.115, f32[384]{0:T(512)S(1)} %fusion.53, f32[384]{0:T(512)S(1)} %get-tuple-element.116, pred[27]{0:T(512)(128)(4,1)S(1)} %get-tuple-element.139), kind=kOutput, calls=%fused_computation.12.clone.1 | convolution fusion | flops 1039171584 | bytes 18680864 | tf_op jit(solution)/shard_map/while/body/eval_jaxpr/qok,okd->qd/dot_general | solution.py:113
  782.8 9.9 select_reduce_fusion.2
  792.7 9.3 fusion.53
  802.0 10.4 %fusion.54 = bf16[1,384,128]{2,1,0:T(8,128)(2,1)S(1)} fusion(bf16[27,384,6,128]{1,3,2,0:T(8,128)(2,1)} %get-tuple-element.143, s32[]{:T(128)S(6)} %select_n.126, f32[384,27,384]{0,2,1:T(8,128)} %get-tuple-element.115, f32[384]{0:T(512)S(1)} %fusion.53, f32[384]{0:T(512)S(1)} %get-tuple-element.116, pred[27]{0:T(512)(128)(4,1)S(1)} %get-tuple-element.139), kind=kOutput, calls=%fused_computation.12.clone.1 | convolution fusion | flops 1039171584 | bytes 18680864 | tf_op jit(solution)/shard_map/while/body/eval_jaxpr/qok,okd->qd/dot_general | solution.py:113
  815.1 9.9 select_reduce_fusion.2
  825.0 9.3 fusion.53
  834.2 10.4 %fusion.54 = bf16[1,384,128]{2,1,0:T(8,128)(2,1)S(1)} fusion(bf16[27,384,6,128]{1,3,2,0:T(8,128)(2,1)} %get-tuple-element.143, s32[]{:T(128)S(6)} %select_n.126, f32[384,27,384]{0,2,1:T(8,128)} %get-tuple-element.115, f32[384]{0:T(512)S(1)} %fusion.53, f32[384]{0:T(512)S(1)} %get-tuple-element.116, pred[27]{0:T(512)(128)(4,1)S(1)} %get-tuple-element.139), kind=kOutput, calls=%fused_computation.12.clone.1 | convolution fusion | flops 1039171584 | bytes 18680864 | tf_op jit(solution)/shard_map/while/body/eval_jaxpr/qok,okd->qd/dot_general | solution.py:113
  847.3 9.9 select_reduce_fusion.2
  857.2 9.3 fusion.53
  866.5 10.4 %fusion.54 = bf16[1,384,128]{2,1,0:T(8,128)(2,1)S(1)} fusion(bf16[27,384,6,128]{1,3,2,0:T(8,128)(2,1)} %get-tuple-element.143, s32[]{:T(128)S(6)} %select_n.126, f32[384,27,384]{0,2,1:T(8,128)} %get-tuple-element.115, f32[384]{0:T(512)S(1)} %fusion.53, f32[384]{0:T(512)S(1)} %get-tuple-element.116, pred[27]{0:T(512)(128)(4,1)S(1)} %get-tuple-element.139), kind=kOutput, calls=%fused_computation.12.clone.1 | convolution fusion | flops 1039171584 | bytes 18680864 | tf_op jit(solution)/shard_map/while/body/eval_jaxpr/qok,okd->qd/dot_general | solution.py:113
  879.6 9.9 select_reduce_fusion.2
  889.5 9.3 fusion.53
  898.8 10.4 %fusion.54 = bf16[1,384,128]{2,1,0:T(8,128)(2,1)S(1)} fusion(bf16[27,384,6,128]{1,3,2,0:T(8,128)(2,1)} %get-tuple-element.143, s32[]{:T(128)S(6)} %select_n.126, f32[384,27,384]{0,2,1:T(8,128)} %get-tuple-element.115, f32[384]{0:T(512)S(1)} %fusion.53, f32[384]{0:T(512)S(1)} %get-tuple-element.116, pred[27]{0:T(512)(128)(4,1)S(1)} %get-tuple-element.139), kind=kOutput, calls=%fused_computation.12.clone.1 | convolution fusion | flops 1039171584 | bytes 18680864 | tf_op jit(solution)/shard_map/while/body/eval_jaxpr/qok,okd->qd/dot_general | solution.py:113
  909.3 5.8 convolution_convert_fusion
  915.2 86.5 %reduce-scatter.2.cloned.1.call-done = bf16[192,3072]{1,0:T(8,128)(2,1)} async-done(((bf16[384,3072]{1,0:T(8,128)(2,1)}), bf16[192,3072]{1,0:T(8,128)(2,1)}) %reduce-scatter.2.cloned.1.call-update) | async-done | bytes 1179664 | tf_op jit(solution)/shard_map/reduce_scatter | solution.py:119
  1001.7 2.5 fusion.33
  (93 shorter events, 21.7 us)
Async XLA Ops:
  6.5 6.9 copy-start
  6.5 50.3 %all-gather.2.cloned.1.call-start = ((), (), s32[]{:S(2)}) async-start(), calls=%async_computation.1 | async-start | bytes 3538944 | tf_op jit(solution)/shard_map/all_gather | solution.py:86
  13.4 988.3 %reduce-scatter.2.cloned.1.call-start = ((), (), s32[]{:S(2)}) async-start(), calls=%async_computation.2 | async-start | bytes 3538944 | tf_op jit(solution)/shard_map/reduce_scatter | solution.py:119
  69.2 18.8 %copy-start.5 = (s32[1,27]{1,0:T(1,128)S(1)}, s32[1,27]{1,0:T(1,128)}, u32[]{:S(2)}) copy-start(s32[1,27]{1,0:T(1,128)} %param.19) | copy-start | bytes 328
  69.2 21.8 %copy-start.4 = (f32[128]{0:T(128)S(1)}, f32[128]{0:T(128)}, u32[]{:S(2)}) copy-start(f32[128]{0:T(128)} %param.14) | copy-start | bytes 1540
  70.8 27.9 %collective-permute-start = (bf16[1,384,1536]{1,2,0:T(8,128)(2,1)}, bf16[1,384,1536]{1,2,0:T(8,128)(2,1)}, u32[]{:S(2)}, u32[]{:S(2)}) collective-permute-start(bf16[1,384,1536]{1,2,0:T(8,128)(2,1)} %maximum_bitcast_fusion), channel_id=1, source_target_pairs={{0,21},{1,22},{2,23},{3,24},{4,25},{5,26},{6,27},{7,28},{8,29},{9,... | collective-permute-start | bytes 3538952 | tf_op jit(solution)/shard_map/ppermute | solution.py:12
  79.3 44.8 %collective-permute-start.1 = (bf16[1,384,1536]{1,2,0:T(8,128)(2,1)}, bf16[1,384,1536]{1,2,0:T(8,128)(2,1)}, u32[]{:S(2)}, u32[]{:S(2)}) collective-permute-start(bf16[1,384,1536]{1,2,0:T(8,128)(2,1)} %maximum_bitcast_fusion), channel_id=1, source_target_pairs={{0,20},{1,21},{2,22},{3,23},{4,24},{5,25},{6,26},{7,27},{8,28},{9,... | collective-permute-start | bytes 3538952 | tf_op jit(solution)/shard_map/ppermute | solution.py:12
  81.9 91.1 %collective-permute-start.2 = (bf16[1,384,1536]{1,2,0:T(8,128)(2,1)}, bf16[1,384,1536]{1,2,0:T(8,128)(2,1)}, u32[]{:S(2)}, u32[]{:S(2)}) collective-permute-start(bf16[1,384,1536]{1,2,0:T(8,128)(2,1)} %maximum_bitcast_fusion), channel_id=1, source_target_pairs={{0,19},{1,20},{2,21},{3,22},{4,23},{5,24},{6,25},{7,26},{8,27},{9,... | collective-permute-start | bytes 3538952 | tf_op jit(solution)/shard_map/ppermute | solution.py:12
  88.0 108.4 %collective-permute-start.3 = (bf16[1,384,1536]{1,2,0:T(8,128)(2,1)}, bf16[1,384,1536]{1,2,0:T(8,128)(2,1)S(1)}, u32[]{:S(2)}, u32[]{:S(2)}) collective-permute-start(bf16[1,384,1536]{1,2,0:T(8,128)(2,1)} %maximum_bitcast_fusion), channel_id=1, source_target_pairs={{0,17},{1,18},{2,19},{3,20},{4,21},{5,22},{6,23},{7,24},{8,25},{9,... | collective-permute-start | bytes 3538952 | tf_op jit(solution)/shard_map/ppermute | solution.py:12
  89.4 146.7 %collective-permute-start.4 = (bf16[1,384,1536]{1,2,0:T(8,128)(2,1)}, bf16[1,384,1536]{1,2,0:T(8,128)(2,1)S(1)}, u32[]{:S(2)}, u32[]{:S(2)}) collective-permute-start(bf16[1,384,1536]{1,2,0:T(8,128)(2,1)} %maximum_bitcast_fusion), channel_id=1, source_target_pairs={{0,16},{1,17},{2,18},{3,19},{4,20},{5,21},{6,22},{7,23},{8,24},{9,... | collective-permute-start | bytes 3538952 | tf_op jit(solution)/shard_map/ppermute | solution.py:12
  98.7 238.0 %collective-permute-start.5 = (bf16[1,384,1536]{1,2,0:T(8,128)(2,1)}, bf16[1,384,1536]{1,2,0:T(8,128)(2,1)S(1)}, u32[]{:S(2)}, u32[]{:S(2)}) collective-permute-start(bf16[1,384,1536]{1,2,0:T(8,128)(2,1)} %maximum_bitcast_fusion), channel_id=1, source_target_pairs={{0,15},{1,16},{2,17},{3,18},{4,19},{5,20},{6,21},{7,22},{8,23},{9,... | collective-permute-start | bytes 3538952 | tf_op jit(solution)/shard_map/ppermute | solution.py:12
  124.2 214.2 %collective-permute-start.6 = (bf16[1,384,1536]{1,2,0:T(8,128)(2,1)}, bf16[1,384,1536]{1,2,0:T(8,128)(2,1)S(1)}, u32[]{:S(2)}, u32[]{:S(2)}) collective-permute-start(bf16[1,384,1536]{1,2,0:T(8,128)(2,1)} %maximum_bitcast_fusion), channel_id=1, source_target_pairs={{0,13},{1,14},{2,15},{3,16},{4,17},{5,18},{6,19},{7,20},{8,21},{9,... | collective-permute-start | bytes 3538952 | tf_op jit(solution)/shard_map/ppermute | solution.py:12
  173.0 167.0 %collective-permute-start.7 = (bf16[1,384,1536]{1,2,0:T(8,128)(2,1)}, bf16[1,384,1536]{1,2,0:T(8,128)(2,1)S(1)}, u32[]{:S(2)}, u32[]{:S(2)}) collective-permute-start(bf16[1,384,1536]{1,2,0:T(8,128)(2,1)} %maximum_bitcast_fusion), channel_id=1, source_target_pairs={{0,12},{1,13},{2,14},{3,15},{4,16},{5,17},{6,18},{7,19},{8,20},{9,... | collective-permute-start | bytes 3538952 | tf_op jit(solution)/shard_map/ppermute | solution.py:12
  196.4 147.1 %collective-permute-start.8 = (bf16[1,384,1536]{1,2,0:T(8,128)(2,1)}, bf16[1,384,1536]{1,2,0:T(8,128)(2,1)S(1)}, u32[]{:S(2)}, u32[]{:S(2)}) collective-permute-start(bf16[1,384,1536]{1,2,0:T(8,128)(2,1)} %maximum_bitcast_fusion), channel_id=1, source_target_pairs={{0,11},{1,12},{2,13},{3,14},{4,15},{5,16},{6,17},{7,18},{8,19},{9,... | collective-permute-start | bytes 3538952 | tf_op jit(solution)/shard_map/ppermute | solution.py:12
  236.1 141.3 %collective-permute-start.9 = (bf16[1,384,1536]{1,2,0:T(8,128)(2,1)}, bf16[1,384,1536]{1,2,0:T(8,128)(2,1)S(1)}, u32[]{:S(2)}, u32[]{:S(2)}) collective-permute-start(bf16[1,384,1536]{1,2,0:T(8,128)(2,1)} %maximum_bitcast_fusion), channel_id=1, source_target_pairs={{0,5},{1,6},{2,7},{3,8},{4,9},{5,10},{6,11},{7,12},{8,13},{9,14},{... | collective-permute-start | bytes 3538952 | tf_op jit(solution)/shard_map/ppermute | solution.py:12
  336.7 42.2 %collective-permute-start.10 = (bf16[1,384,1536]{1,2,0:T(8,128)(2,1)}, bf16[1,384,1536]{1,2,0:T(8,128)(2,1)S(1)}, u32[]{:S(2)}, u32[]{:S(2)}) collective-permute-start(bf16[1,384,1536]{1,2,0:T(8,128)(2,1)} %maximum_bitcast_fusion), channel_id=1, source_target_pairs={{0,4},{1,5},{2,6},{3,7},{4,8},{5,9},{6,10},{7,11},{8,12},{9,13},{1... | collective-permute-start | bytes 3538952 | tf_op jit(solution)/shard_map/ppermute | solution.py:12
  338.3 45.1 %collective-permute-start.11 = (bf16[1,384,1536]{1,2,0:T(8,128)(2,1)}, bf16[1,384,1536]{1,2,0:T(8,128)(2,1)S(1)}, u32[]{:S(2)}, u32[]{:S(2)}) collective-permute-start(bf16[1,384,1536]{1,2,0:T(8,128)(2,1)} %maximum_bitcast_fusion), channel_id=1, source_target_pairs={{0,3},{1,4},{2,5},{3,6},{4,7},{5,8},{6,9},{7,10},{8,11},{9,12},{10... | collective-permute-start | bytes 3538952 | tf_op jit(solution)/shard_map/ppermute | solution.py:12
  340.0 56.1 %collective-permute-start.12 = (bf16[1,384,1536]{1,2,0:T(8,128)(2,1)}, bf16[1,384,1536]{1,2,0:T(8,128)(2,1)S(1)}, u32[]{:S(2)}, u32[]{:S(2)}) collective-permute-start(bf16[1,384,1536]{1,2,0:T(8,128)(2,1)} %maximum_bitcast_fusion), channel_id=1, source_target_pairs={{0,1},{1,2},{2,3},{3,4},{4,5},{5,6},{6,7},{7,8},{8,9},{9,10},{10,1... | collective-permute-start | bytes 3538952 | tf_op jit(solution)/shard_map/ppermute | solution.py:12
  343.6 56.8 %collective-permute-start.13 = (bf16[1,384,1536]{1,2,0:T(8,128)(2,1)}, bf16[1,384,1536]{1,2,0:T(8,128)(2,1)S(1)}, u32[]{:S(2)}, u32[]{:S(2)}) collective-permute-start(bf16[1,384,1536]{1,2,0:T(8,128)(2,1)} %maximum_bitcast_fusion), channel_id=1, source_target_pairs={{1,0},{2,1},{3,2},{4,3},{5,4},{6,5},{7,6},{8,7},{9,8},{10,9},{11,1... | collective-permute-start | bytes 3538952 | tf_op jit(solution)/shard_map/ppermute | solution.py:12
  377.4 64.1 %collective-permute-start.14 = (bf16[1,384,1536]{1,2,0:T(8,128)(2,1)}, bf16[1,384,1536]{1,2,0:T(8,128)(2,1)S(1)}, u32[]{:S(2)}, u32[]{:S(2)}) collective-permute-start(bf16[1,384,1536]{1,2,0:T(8,128)(2,1)} %maximum_bitcast_fusion), channel_id=1, source_target_pairs={{3,0},{4,1},{5,2},{6,3},{7,4},{8,5},{9,6},{10,7},{11,8},{12,9},{13... | collective-permute-start | bytes 3538952 | tf_op jit(solution)/shard_map/ppermute | solution.py:12
  378.9 64.1 %collective-permute-start.15 = (bf16[1,384,1536]{1,2,0:T(8,128)(2,1)}, bf16[1,384,1536]{1,2,0:T(8,128)(2,1)S(1)}, u32[]{:S(2)}, u32[]{:S(2)}) collective-permute-start(bf16[1,384,1536]{1,2,0:T(8,128)(2,1)} %maximum_bitcast_fusion), channel_id=1, source_target_pairs={{4,0},{5,1},{6,2},{7,3},{8,4},{9,5},{10,6},{11,7},{12,8},{13,9},{1... | collective-permute-start | bytes 3538952 | tf_op jit(solution)/shard_map/ppermute | solution.py:12
  383.4 96.2 %collective-permute-start.16 = (bf16[1,384,1536]{1,2,0:T(8,128)(2,1)}, bf16[1,384,1536]{1,2,0:T(8,128)(2,1)S(1)}, u32[]{:S(2)}, u32[]{:S(2)}) collective-permute-start(bf16[1,384,1536]{1,2,0:T(8,128)(2,1)} %maximum_bitcast_fusion), channel_id=1, source_target_pairs={{5,0},{6,1},{7,2},{8,3},{9,4},{10,5},{11,6},{12,7},{13,8},{14,9},{... | collective-permute-start | bytes 3538952 | tf_op jit(solution)/shard_map/ppermute | solution.py:12
  396.1 93.0 %collective-permute-start.17 = (bf16[1,384,1536]{1,2,0:T(8,128)(2,1)}, bf16[1,384,1536]{1,2,0:T(8,128)(2,1)S(1)}, u32[]{:S(2)}, u32[]{:S(2)}) collective-permute-start(bf16[1,384,1536]{1,2,0:T(8,128)(2,1)} %maximum_bitcast_fusion), channel_id=1, source_target_pairs={{11,0},{12,1},{13,2},{14,3},{15,4},{16,5},{17,6},{18,7},{19,8},{20... | collective-permute-start | bytes 3538952 | tf_op jit(solution)/shard_map/ppermute | solution.py:12
  400.4 103.9 %collective-permute-start.18 = (bf16[1,384,1536]{1,2,0:T(8,128)(2,1)}, bf16[1,384,1536]{1,2,0:T(8,128)(2,1)S(1)}, u32[]{:S(2)}, u32[]{:S(2)}) collective-permute-start(bf16[1,384,1536]{1,2,0:T(8,128)(2,1)} %maximum_bitcast_fusion), channel_id=1, source_target_pairs={{12,0},{13,1},{14,2},{15,3},{16,4},{17,5},{18,6},{19,7},{20,8},{21... | collective-permute-start | bytes 3538952 | tf_op jit(solution)/shard_map/ppermute | solution.py:12
  441.5 108.0 %collective-permute-start.19 = (bf16[1,384,1536]{1,2,0:T(8,128)(2,1)}, bf16[1,384,1536]{1,2,0:T(8,128)(2,1)S(1)}, u32[]{:S(2)}, u32[]{:S(2)}) collective-permute-start(bf16[1,384,1536]{1,2,0:T(8,128)(2,1)} %maximum_bitcast_fusion), channel_id=1, source_target_pairs={{13,0},{14,1},{15,2},{16,3},{17,4},{18,5},{19,6},{20,7},{21,8},{22... | collective-permute-start | bytes 3538952 | tf_op jit(solution)/shard_map/ppermute | solution.py:12
  443.1 107.9 %collective-permute-start.20 = (bf16[1,384,1536]{1,2,0:T(8,128)(2,1)}, bf16[1,384,1536]{1,2,0:T(8,128)(2,1)S(1)}, u32[]{:S(2)}, u32[]{:S(2)}) collective-permute-start(bf16[1,384,1536]{1,2,0:T(8,128)(2,1)} %maximum_bitcast_fusion), channel_id=1, source_target_pairs={{15,0},{16,1},{17,2},{18,3},{19,4},{20,5},{21,6},{22,7},{23,8},{24... | collective-permute-start | bytes 3538952 | tf_op jit(solution)/shard_map/ppermute | solution.py:12
  479.6 72.9 %collective-permute-start.21 = (bf16[1,384,1536]{1,2,0:T(8,128)(2,1)}, bf16[1,384,1536]{1,2,0:T(8,128)(2,1)S(1)}, u32[]{:S(2)}, u32[]{:S(2)}) collective-permute-start(bf16[1,384,1536]{1,2,0:T(8,128)(2,1)} %maximum_bitcast_fusion), channel_id=1, source_target_pairs={{16,0},{17,1},{18,2},{19,3},{20,4},{21,5},{22,6},{23,7},{24,8},{25... | collective-permute-start | bytes 3538952 | tf_op jit(solution)/shard_map/ppermute | solution.py:12
  489.1 68.5 %collective-permute-start.22 = (bf16[1,384,1536]{1,2,0:T(8,128)(2,1)}, bf16[1,384,1536]{1,2,0:T(8,128)(2,1)S(1)}, u32[]{:S(2)}, u32[]{:S(2)}) collective-permute-start(bf16[1,384,1536]{1,2,0:T(8,128)(2,1)} %maximum_bitcast_fusion), channel_id=1, source_target_pairs={{17,0},{18,1},{19,2},{20,3},{21,4},{22,5},{23,6},{24,7},{25,8},{26... | collective-permute-start | bytes 3538952 | tf_op jit(solution)/shard_map/ppermute | solution.py:12
  504.3 144.5 %collective-permute-start.23 = (bf16[1,384,1536]{1,2,0:T(8,128)(2,1)}, bf16[1,384,1536]{1,2,0:T(8,128)(2,1)S(1)}, u32[]{:S(2)}, u32[]{:S(2)}) collective-permute-start(bf16[1,384,1536]{1,2,0:T(8,128)(2,1)} %maximum_bitcast_fusion), channel_id=1, source_target_pairs={{19,0},{20,1},{21,2},{22,3},{23,4},{24,5},{25,6},{26,7},{27,8},{28... | collective-permute-start | bytes 3538952 | tf_op jit(solution)/shard_map/ppermute | solution.py:12
  549.5 99.6 %collective-permute-start.24 = (bf16[1,384,1536]{1,2,0:T(8,128)(2,1)}, bf16[1,384,1536]{1,2,0:T(8,128)(2,1)S(1)}, u32[]{:S(2)}, u32[]{:S(2)}) collective-permute-start(bf16[1,384,1536]{1,2,0:T(8,128)(2,1)} %maximum_bitcast_fusion), channel_id=1, source_target_pairs={{20,0},{21,1},{22,2},{23,3},{24,4},{25,5},{26,6},{27,7},{28,8},{29... | collective-permute-start | bytes 3538952 | tf_op jit(solution)/shard_map/ppermute | solution.py:12
  551.0 153.7 %collective-permute-start.25 = (bf16[1,384,1536]{1,2,0:T(8,128)(2,1)}, bf16[1,384,1536]{1,2,0:T(8,128)(2,1)S(1)}, u32[]{:S(2)}, u32[]{:S(2)}) collective-permute-start(bf16[1,384,1536]{1,2,0:T(8,128)(2,1)} %maximum_bitcast_fusion), channel_id=1, source_target_pairs={{21,0},{22,1},{23,2},{24,3},{25,4},{26,5},{27,6},{28,7},{29,8},{30... | collective-permute-start | bytes 3538952 | tf_op jit(solution)/shard_map/ppermute | solution.py:12
  704.9 10.8 %copy-start.2 = (bf16[6,384,128]{1,2,0:T(8,128)(2,1)S(1)}, bf16[6,384,128]{1,2,0:T(8,128)(2,1)}, u32[]{:S(2)}) copy-start(bf16[6,384,128]{1,2,0:T(8,128)(2,1)} %custom-call.1) | copy-start | bytes 1769476
  909.3 92.4 %copy-start.3 = (f32[3072]{0:T(1024)S(1)}, f32[3072]{0:T(1024)}, u32[]{:S(2)}) copy-start(f32[3072]{0:T(1024)} %param.18) | copy-start | bytes 36868
  909.3 94.9 %copy-start.1 = (f32[128]{0:T(128)S(1)}, f32[128]{0:T(128)}, u32[]{:S(2)}) copy-start(f32[128]{0:T(128)} %param.15) | copy-start | bytes 1540
Sparse Core Ops, SparseCore 0:
  13.5 43.2 all-gather.1
  915.3 86.3 reduce-scatter.1
where the time goes:
time: 1010 us
  waiting for transfers between devices  477 us (47%)
  starting transfers between devices  276 us (27%)
  matrix products  139 us (14%)
  other arithmetic  67.1 us (7%)
  local copies, waits for them, and re-layouts  26.2 us (3%)
  between operations  14 us (1%)
  loops' own time  11.9 us (1%)
    ppermute x26, waiting for transfers between devices, shifted(): lax.ppermute(value, axis, [(source, source + steps) for source in range(l...  347 us
    ppermute x26, starting transfers between devices, shifted(): lax.ppermute(value, axis, [(source, source + steps) for source in range(l...  276 us
    reduce_scatter x1, waiting for transfers between devices, on_device(): lax.psum_scatter(jnp.dot(attention, out_weight, preferred_element_type=jn...  86.5 us
    dot_general x6, matrix products, one_head(): jnp.einsum('qok,okd->qd', weights, value_rows, preferred_element_type=jnp...  62.2 us
    dot_general x6, matrix products, one_head(): jnp.einsum('qd,okd->qok', query_rows, key_rows, preferred_element_type=jn...  59.5 us
    reduce_sum x6, other arithmetic, soft_weights(): jnp.sum(raised, axis=(1, 2), keepdims=True)  55.5 us
    all_gather x1, waiting for transfers between devices, on_device(): lax.all_gather(normed, 'heads', axis=0, tiled=True)  43.4 us
  transfers between devices with their start and end apart: 28, of which 15 were waited for; matrix products, arithmetic and copies ran while one was open for 1% of the time, Pallas kernels for 0%

commit v1 on v0

--- a/solution.py
+++ b/solution.py
@@ -83,7 +83,9 @@
     group_heads = group_width // head_dim
     normed = modulate(tokens[0], mod_shift, mod_scale)
     projected = jnp.dot(
-        lax.all_gather(normed, "heads", axis=0, tiled=True),
+        jnp.concatenate(
+            lax.all_to_all(jnp.stack([normed] * lax.axis_size("heads")), "heads", 0, 0), axis=0
+        ),
         qkv_weight,
         preferred_element_type=jnp.float32,
     ).astype(jnp.bfloat16)

time: 1010 us -> 1020 us (level)
    reduce_scatter x1, waiting for transfers between devices: 86.5 us -> 134 us  [on_device(): lax.psum_scatter(jnp.dot(attention, out_weight, preferred_element_type=jn...]
    all_gather x1 -> x0, waiting for transfers between devices: 43.4 us -> none  [on_device(): lax.all_gather(normed, 'heads', axis=0, tiled=True)]
    ppermute x26, waiting for transfers between devices: 347 us -> 312 us  [shifted(): lax.ppermute(value, axis, [(source, source + steps) for source in range(l...]
    all_to_all x0 -> x1, waiting for transfers between devices: none -> 28.3 us  [on_device(): lax.all_to_all(jnp.stack([normed] * lax.axis_size('heads')), 'heads', 0, 0)]
where the time goes in v1:
time: 1020 us
  waiting for transfers between devices  474 us (46%)
  starting transfers between devices  286 us (28%)
  matrix products  138 us (14%)
  other arithmetic  67.2 us (7%)
  local copies, waits for them, and re-layouts  27.9 us (3%)
  between operations  14 us (1%)
  loops' own time  11.9 us (1%)
    ppermute x26, waiting for transfers between devices, shifted(): lax.ppermute(value, axis, [(source, source + steps) for source in range(l...  312 us
    ppermute x26, starting transfers between devices, shifted(): lax.ppermute(value, axis, [(source, source + steps) for source in range(l...  280 us
    reduce_scatter x1, waiting for transfers between devices, on_device(): lax.psum_scatter(jnp.dot(attention, out_weight, preferred_element_type=jn...  134 us
    dot_general x6, matrix products, one_head(): jnp.einsum('qok,okd->qd', weights, value_rows, preferred_element_type=jnp...  62.2 us
    dot_general x6, matrix products, one_head(): jnp.einsum('qd,okd->qok', query_rows, key_rows, preferred_element_type=jn...  59.5 us
    reduce_sum x6, other arithmetic, soft_weights(): jnp.sum(raised, axis=(1, 2), keepdims=True)  55.5 us
    all_to_all x1, waiting for transfers between devices, on_device(): lax.all_to_all(jnp.stack([normed] * lax.axis_size('heads')), 'heads', 0, 0)  28.3 us
  transfers between devices with their start and end apart: 28, of which 15 were waited for; matrix products, arithmetic and copies ran while one was open for 1% of the time, Pallas kernels for 0%

profile of v1, /device:TPU:1, one launch (start us, length us, event | category | flops | bytes accessed | tf_op | source)
XLA Modules:
  0.0 1018.5 jit_solution(16637109274758059174)
XLA Ops:
  7.3 1.5 convert_reduce_fusion
  8.9 1.7 fusion.28
  11.9 1.6 pad_maximum_fusion
  13.5 5.7 all-to-all-start
  19.2 28.3 %all-to-all-done = bf16[2,192,3072]{2,1,0:T(8,128)(2,1)S(1)} async-done(((bf16[2,192,3072]{2,1,0:T(8,128)(2,1)}), bf16[2,192,3072]{2,1,0:T(8,128)(2,1)S(1)}, u32[]{:S(2)}, u32[]{:S(2)}) %all-to-all-start) | async-done | bytes 2359328 | tf_op jit(solution)/shard_map/all_to_all | solution.py:87
  47.5 10.2 %convolution_convert_fusion.1 = bf16[384,2304]{1,0:T(8,128)(2,1)} fusion(bf16[384,3072]{1,0:T(8,128)(2,1)S(1)} %bitcast.99, bf16[3072,2304]{1,0:T(8,128)(2,1)} %param.12), kind=kOutput, calls=%fused_computation.21 | convolution fusion | flops 5436702720 | bytes 18284544 | tf_op jit(solution)/shard_map/dot_general | solution.py:85
  57.7 2.8 copy.14
  62.1 9.7 collective-permute-start
  71.9 2.7 collective-permute-start.1
  74.6 5.3 collective-permute-start.2
  80.0 1.4 collective-permute-start.3
  81.4 2.2 collective-permute-start.4
  83.9 7.3 collective-permute-done
  91.2 21.4 %collective-permute-start.5 = (bf16[1,384,1536]{1,2,0:T(8,128)(2,1)}, bf16[1,384,1536]{1,2,0:T(8,128)(2,1)S(1)}, u32[]{:S(2)}, u32[]{:S(2)}) collective-permute-start(bf16[1,384,1536]{1,2,0:T(8,128)(2,1)} %maximum_bitcast_fusion), channel_id=1, source_target_pairs={{0,15},{1,16},{2,17},{3,18},{4,19},{5,20},{6,21},{7,22},{8,23},{9,... | collective-permute-start | bytes 3538952 | tf_op jit(solution)/shard_map/ppermute | solution.py:12
  112.6 1.4 constant_dynamic-update-slice_fusion.27
  114.0 48.3 %collective-permute-start.6 = (bf16[1,384,1536]{1,2,0:T(8,128)(2,1)}, bf16[1,384,1536]{1,2,0:T(8,128)(2,1)S(1)}, u32[]{:S(2)}, u32[]{:S(2)}) collective-permute-start(bf16[1,384,1536]{1,2,0:T(8,128)(2,1)} %maximum_bitcast_fusion), channel_id=1, source_target_pairs={{0,13},{1,14},{2,15},{3,16},{4,17},{5,18},{6,19},{7,20},{8,21},{9,... | collective-permute-start | bytes 3538952 | tf_op jit(solution)/shard_map/ppermute | solution.py:12
  162.3 1.5 constant_dynamic-update-slice_fusion.26
  163.8 24.3 %collective-permute-start.7 = (bf16[1,384,1536]{1,2,0:T(8,128)(2,1)}, bf16[1,384,1536]{1,2,0:T(8,128)(2,1)S(1)}, u32[]{:S(2)}, u32[]{:S(2)}) collective-permute-start(bf16[1,384,1536]{1,2,0:T(8,128)(2,1)} %maximum_bitcast_fusion), channel_id=1, source_target_pairs={{0,12},{1,13},{2,14},{3,15},{4,16},{5,17},{6,18},{7,19},{8,20},{9,... | collective-permute-start | bytes 3538952 | tf_op jit(solution)/shard_map/ppermute | solution.py:12
  188.1 1.5 constant_dynamic-update-slice_fusion.25
  189.7 38.3 %collective-permute-start.8 = (bf16[1,384,1536]{1,2,0:T(8,128)(2,1)}, bf16[1,384,1536]{1,2,0:T(8,128)(2,1)S(1)}, u32[]{:S(2)}, u32[]{:S(2)}) collective-permute-start(bf16[1,384,1536]{1,2,0:T(8,128)(2,1)} %maximum_bitcast_fusion), channel_id=1, source_target_pairs={{0,11},{1,12},{2,13},{3,14},{4,15},{5,16},{6,17},{7,18},{8,19},{9,... | collective-permute-start | bytes 3538952 | tf_op jit(solution)/shard_map/ppermute | solution.py:12
  228.2 103.0 %collective-permute-start.9 = (bf16[1,384,1536]{1,2,0:T(8,128)(2,1)}, bf16[1,384,1536]{1,2,0:T(8,128)(2,1)S(1)}, u32[]{:S(2)}, u32[]{:S(2)}) collective-permute-start(bf16[1,384,1536]{1,2,0:T(8,128)(2,1)} %maximum_bitcast_fusion), channel_id=1, source_target_pairs={{0,5},{1,6},{2,7},{3,8},{4,9},{5,10},{6,11},{7,12},{8,13},{9,14},{... | collective-permute-start | bytes 3538952 | tf_op jit(solution)/shard_map/ppermute | solution.py:12
  331.5 1.4 collective-permute-start.10
  333.1 1.4 collective-permute-start.11
  334.7 3.3 collective-permute-start.12
  338.3 1.9 collective-permute-start.13
  340.5 31.9 %collective-permute-done.9 = bf16[1,384,1536]{1,2,0:T(8,128)(2,1)S(1)} collective-permute-done((bf16[1,384,1536]{1,2,0:T(8,128)(2,1)}, bf16[1,384,1536]{1,2,0:T(8,128)(2,1)S(1)}, u32[]{:S(2)}, u32[]{:S(2)}) %collective-permute-start.9) | collective-permute-done | bytes 1179680 | tf_op jit(solution)/shard_map/ppermute | solution.py:12
  373.9 1.3 collective-permute-start.15
  377.1 11.1 %collective-permute-done.12 = bf16[1,384,1536]{1,2,0:T(8,128)(2,1)S(1)} collective-permute-done((bf16[1,384,1536]{1,2,0:T(8,128)(2,1)}, bf16[1,384,1536]{1,2,0:T(8,128)(2,1)S(1)}, u32[]{:S(2)}, u32[]{:S(2)}) %collective-permute-start.12) | collective-permute-done | bytes 1179680 | tf_op jit(solution)/shard_map/ppermute | solution.py:12
  390.0 4.1 collective-permute-done.13
  394.0 1.3 collective-permute-start.18
  395.6 38.6 %collective-permute-done.14 = bf16[1,384,1536]{1,2,0:T(8,128)(2,1)S(1)} collective-permute-done((bf16[1,384,1536]{1,2,0:T(8,128)(2,1)}, bf16[1,384,1536]{1,2,0:T(8,128)(2,1)S(1)}, u32[]{:S(2)}, u32[]{:S(2)}) %collective-permute-start.14) | collective-permute-done | bytes 1179680 | tf_op jit(solution)/shard_map/ppermute | solution.py:12
  434.2 1.5 collective-permute-start.19
  435.9 1.3 collective-permute-start.20
  437.4 34.9 %collective-permute-done.16 = bf16[1,384,1536]{1,2,0:T(8,128)(2,1)S(1)} collective-permute-done((bf16[1,384,1536]{1,2,0:T(8,128)(2,1)}, bf16[1,384,1536]{1,2,0:T(8,128)(2,1)S(1)}, u32[]{:S(2)}, u32[]{:S(2)}) %collective-permute-start.16) | collective-permute-done | bytes 1179680 | tf_op jit(solution)/shard_map/ppermute | solution.py:12
  473.8 9.4 collective-permute-done.17
  484.8 11.4 %collective-permute-done.18 = bf16[1,384,1536]{1,2,0:T(8,128)(2,1)S(1)} collective-permute-done((bf16[1,384,1536]{1,2,0:T(8,128)(2,1)}, bf16[1,384,1536]{1,2,0:T(8,128)(2,1)S(1)}, u32[]{:S(2)}, u32[]{:S(2)}) %collective-permute-start.18) | collective-permute-done | bytes 1179680 | tf_op jit(solution)/shard_map/ppermute | solution.py:12
  497.7 44.3 %collective-permute-done.19 = bf16[1,384,1536]{1,2,0:T(8,128)(2,1)S(1)} collective-permute-done((bf16[1,384,1536]{1,2,0:T(8,128)(2,1)}, bf16[1,384,1536]{1,2,0:T(8,128)(2,1)S(1)}, u32[]{:S(2)}, u32[]{:S(2)}) %collective-permute-start.19) | collective-permute-done | bytes 1179680 | tf_op jit(solution)/shard_map/ppermute | solution.py:12
  543.6 1.3 collective-permute-start.25
  545.4 8.4 collective-permute-done.22
  554.0 71.5 %collective-permute-done.23 = bf16[1,384,1536]{1,2,0:T(8,128)(2,1)S(1)} collective-permute-done((bf16[1,384,1536]{1,2,0:T(8,128)(2,1)}, bf16[1,384,1536]{1,2,0:T(8,128)(2,1)S(1)}, u32[]{:S(2)}, u32[]{:S(2)}) %collective-permute-start.23) | collective-permute-done | bytes 1179680 | tf_op jit(solution)/shard_map/ppermute | solution.py:12
  626.0 39.2 %collective-permute-done.25 = bf16[1,384,1536]{1,2,0:T(8,128)(2,1)S(1)} collective-permute-done((bf16[1,384,1536]{1,2,0:T(8,128)(2,1)}, bf16[1,384,1536]{1,2,0:T(8,128)(2,1)S(1)}, u32[]{:S(2)}, u32[]{:S(2)}) %collective-permute-start.25) | collective-permute-done | bytes 1179680 | tf_op jit(solution)/shard_map/ppermute | solution.py:12
  665.4 10.8 %fusion.44 = (bf16[27,384,768]{1,2,0:T(8,128)(2,1)}, bf16[27,384,768]{1,2,0:T(8,128)(2,1)}) fusion(bf16[27,384,1536]{1,2,0:T(8,128)(2,1)S(1)} %constant_dynamic-update-slice_fusion.1), kind=kLoop, calls=%fused_computation.99 | loop fusion | bytes 63700992 | tf_op jit(solution)/shard_map/slice | solution.py:106
  676.2 193.5 %while.10 = (s32[]{:T(128)}, bf16[6,384,128]{1,2,0:T(8,128)(2,1)S(1)}, pred[27]{0:T(512)(128)(4,1)S(1)}, s32[6]{0:T(128)S(1)}, bf16[384,6,128]{0,2,1:T(8,128)(2,...) while((s32[]{:T(128)}, ...), condition=%wide.region_7.8_spmd, body=%wide.region_4.7_spmd.sunk | while | flops 2082274560 | bytes 53683416 | solution.py:119
  678.7 9.9 select_reduce_fusion.2
  688.7 9.3 fusion.53
  697.9 10.4 %fusion.54 = bf16[1,384,128]{2,1,0:T(8,128)(2,1)S(1)} fusion(bf16[27,384,6,128]{1,3,2,0:T(8,128)(2,1)} %get-tuple-element.143, s32[]{:T(128)S(6)} %select_n.126, f32[384,27,384]{0,2,1:T(8,128)} %get-tuple-element.115, f32[384]{0:T(512)S(1)} %fusion.53, f32[384]{0:T(512)S(1)} %get-tuple-element.116, pred[27]{0:T(512)(128)(4,1)S(1)} %get-tuple-element.139), kind=kOutput, calls=%fused_computation.12.clone.1 | convolution fusion | flops 1039171584 | bytes 18680864 | tf_op jit(solution)/shard_map/while/body/eval_jaxpr/qok,okd->qd/dot_general | solution.py:115
  711.0 9.9 select_reduce_fusion.2
  720.9 9.3 fusion.53
  730.2 10.4 %fusion.54 = bf16[1,384,128]{2,1,0:T(8,128)(2,1)S(1)} fusion(bf16[27,384,6,128]{1,3,2,0:T(8,128)(2,1)} %get-tuple-element.143, s32[]{:T(128)S(6)} %select_n.126, f32[384,27,384]{0,2,1:T(8,128)} %get-tuple-element.115, f32[384]{0:T(512)S(1)} %fusion.53, f32[384]{0:T(512)S(1)} %get-tuple-element.116, pred[27]{0:T(512)(128)(4,1)S(1)} %get-tuple-element.139), kind=kOutput, calls=%fused_computation.12.clone.1 | convolution fusion | flops 1039171584 | bytes 18680864 | tf_op jit(solution)/shard_map/while/body/eval_jaxpr/qok,okd->qd/dot_general | solution.py:115
  743.2 9.9 select_reduce_fusion.2
  753.2 9.3 fusion.53
  762.4 10.4 %fusion.54 = bf16[1,384,128]{2,1,0:T(8,128)(2,1)S(1)} fusion(bf16[27,384,6,128]{1,3,2,0:T(8,128)(2,1)} %get-tuple-element.143, s32[]{:T(128)S(6)} %select_n.126, f32[384,27,384]{0,2,1:T(8,128)} %get-tuple-element.115, f32[384]{0:T(512)S(1)} %fusion.53, f32[384]{0:T(512)S(1)} %get-tuple-element.116, pred[27]{0:T(512)(128)(4,1)S(1)} %get-tuple-element.139), kind=kOutput, calls=%fused_computation.12.clone.1 | convolution fusion | flops 1039171584 | bytes 18680864 | tf_op jit(solution)/shard_map/while/body/eval_jaxpr/qok,okd->qd/dot_general | solution.py:115
  775.5 9.9 select_reduce_fusion.2
  785.4 9.3 fusion.53
  794.7 10.4 %fusion.54 = bf16[1,384,128]{2,1,0:T(8,128)(2,1)S(1)} fusion(bf16[27,384,6,128]{1,3,2,0:T(8,128)(2,1)} %get-tuple-element.143, s32[]{:T(128)S(6)} %select_n.126, f32[384,27,384]{0,2,1:T(8,128)} %get-tuple-element.115, f32[384]{0:T(512)S(1)} %fusion.53, f32[384]{0:T(512)S(1)} %get-tuple-element.116, pred[27]{0:T(512)(128)(4,1)S(1)} %get-tuple-element.139), kind=kOutput, calls=%fused_computation.12.clone.1 | convolution fusion | flops 1039171584 | bytes 18680864 | tf_op jit(solution)/shard_map/while/body/eval_jaxpr/qok,okd->qd/dot_general | solution.py:115
  807.7 9.9 select_reduce_fusion.2
  817.7 9.3 fusion.53
  826.9 10.4 %fusion.54 = bf16[1,384,128]{2,1,0:T(8,128)(2,1)S(1)} fusion(bf16[27,384,6,128]{1,3,2,0:T(8,128)(2,1)} %get-tuple-element.143, s32[]{:T(128)S(6)} %select_n.126, f32[384,27,384]{0,2,1:T(8,128)} %get-tuple-element.115, f32[384]{0:T(512)S(1)} %fusion.53, f32[384]{0:T(512)S(1)} %get-tuple-element.116, pred[27]{0:T(512)(128)(4,1)S(1)} %get-tuple-element.139), kind=kOutput, calls=%fused_computation.12.clone.1 | convolution fusion | flops 1039171584 | bytes 18680864 | tf_op jit(solution)/shard_map/while/body/eval_jaxpr/qok,okd->qd/dot_general | solution.py:115
  840.0 9.9 select_reduce_fusion.2
  849.9 9.3 fusion.53
  859.2 10.4 %fusion.54 = bf16[1,384,128]{2,1,0:T(8,128)(2,1)S(1)} fusion(bf16[27,384,6,128]{1,3,2,0:T(8,128)(2,1)} %get-tuple-element.143, s32[]{:T(128)S(6)} %select_n.126, f32[384,27,384]{0,2,1:T(8,128)} %get-tuple-element.115, f32[384]{0:T(512)S(1)} %fusion.53, f32[384]{0:T(512)S(1)} %get-tuple-element.116, pred[27]{0:T(512)(128)(4,1)S(1)} %get-tuple-element.139), kind=kOutput, calls=%fused_computation.12.clone.1 | convolution fusion | flops 1039171584 | bytes 18680864 | tf_op jit(solution)/shard_map/while/body/eval_jaxpr/qok,okd->qd/dot_general | solution.py:115
  869.7 5.8 convolution_convert_fusion
  875.6 133.6 %reduce-scatter.2.cloned.1.call-done = bf16[192,3072]{1,0:T(8,128)(2,1)} async-done(((bf16[384,3072]{1,0:T(8,128)(2,1)}), bf16[192,3072]{1,0:T(8,128)(2,1)}) %reduce-scatter.2.cloned.1.call-update) | async-done | bytes 1179664 | tf_op jit(solution)/shard_map/reduce_scatter | solution.py:121
  1009.2 2.5 fusion.33
  (95 shorter events, 23.3 us)
Async XLA Ops:
  6.5 12.7 %copy-start = (f32[128]{0:T(128)S(1)}, f32[128]{0:T(128)}, u32[]{:S(2)}) copy-start(f32[128]{0:T(128)} %param.15) | copy-start | bytes 1540
  6.5 4.1 copy-start.2
  13.5 34.0 %all-to-all-start = ((bf16[2,192,3072]{2,1,0:T(8,128)(2,1)}), bf16[2,192,3072]{2,1,0:T(8,128)(2,1)S(1)}, u32[]{:S(2)}, u32[]{:S(2)}) async-start(bf16[2,192,3072]{2,1,0:T(8,128)(2,1)} %pad_maximum_fusion), calls=%async_computation | async-start | bytes 4718592 | tf_op jit(solution)/shard_map/all_to_all | solution.py:87
  19.2 990.0 %reduce-scatter.2.cloned.1.call-start = ((), (), s32[]{:S(2)}) async-start(), calls=%async_computation.2 | async-start | bytes 3538944 | tf_op jit(solution)/shard_map/reduce_scatter | solution.py:121
  60.6 19.3 %copy-start.6 = (s32[1,27]{1,0:T(1,128)S(1)}, s32[1,27]{1,0:T(1,128)}, u32[]{:S(2)}) copy-start(s32[1,27]{1,0:T(1,128)} %param.19) | copy-start | bytes 328
  60.6 23.1 %copy-start.5 = (f32[128]{0:T(128)S(1)}, f32[128]{0:T(128)}, u32[]{:S(2)}) copy-start(f32[128]{0:T(128)} %param.14) | copy-start | bytes 1540
  62.1 29.1 %collective-permute-start = (bf16[1,384,1536]{1,2,0:T(8,128)(2,1)}, bf16[1,384,1536]{1,2,0:T(8,128)(2,1)}, u32[]{:S(2)}, u32[]{:S(2)}) collective-permute-start(bf16[1,384,1536]{1,2,0:T(8,128)(2,1)} %maximum_bitcast_fusion), channel_id=1, source_target_pairs={{0,21},{1,22},{2,23},{3,24},{4,25},{5,26},{6,27},{7,28},{8,29},{9,... | collective-permute-start | bytes 3538952 | tf_op jit(solution)/shard_map/ppermute | solution.py:12
  71.9 42.1 %collective-permute-start.1 = (bf16[1,384,1536]{1,2,0:T(8,128)(2,1)}, bf16[1,384,1536]{1,2,0:T(8,128)(2,1)}, u32[]{:S(2)}, u32[]{:S(2)}) collective-permute-start(bf16[1,384,1536]{1,2,0:T(8,128)(2,1)} %maximum_bitcast_fusion), channel_id=1, source_target_pairs={{0,20},{1,21},{2,22},{3,23},{4,24},{5,25},{6,26},{7,27},{8,28},{9,... | collective-permute-start | bytes 3538952 | tf_op jit(solution)/shard_map/ppermute | solution.py:12
  74.6 89.2 %collective-permute-start.2 = (bf16[1,384,1536]{1,2,0:T(8,128)(2,1)}, bf16[1,384,1536]{1,2,0:T(8,128)(2,1)}, u32[]{:S(2)}, u32[]{:S(2)}) collective-permute-start(bf16[1,384,1536]{1,2,0:T(8,128)(2,1)} %maximum_bitcast_fusion), channel_id=1, source_target_pairs={{0,19},{1,20},{2,21},{3,22},{4,23},{5,24},{6,25},{7,26},{8,27},{9,... | collective-permute-start | bytes 3538952 | tf_op jit(solution)/shard_map/ppermute | solution.py:12
  80.0 109.7 %collective-permute-start.3 = (bf16[1,384,1536]{1,2,0:T(8,128)(2,1)}, bf16[1,384,1536]{1,2,0:T(8,128)(2,1)S(1)}, u32[]{:S(2)}, u32[]{:S(2)}) collective-permute-start(bf16[1,384,1536]{1,2,0:T(8,128)(2,1)} %maximum_bitcast_fusion), channel_id=1, source_target_pairs={{0,17},{1,18},{2,19},{3,20},{4,21},{5,22},{6,23},{7,24},{8,25},{9,... | collective-permute-start | bytes 3538952 | tf_op jit(solution)/shard_map/ppermute | solution.py:12
  81.4 146.9 %collective-permute-start.4 = (bf16[1,384,1536]{1,2,0:T(8,128)(2,1)}, bf16[1,384,1536]{1,2,0:T(8,128)(2,1)S(1)}, u32[]{:S(2)}, u32[]{:S(2)}) collective-permute-start(bf16[1,384,1536]{1,2,0:T(8,128)(2,1)} %maximum_bitcast_fusion), channel_id=1, source_target_pairs={{0,16},{1,17},{2,18},{3,19},{4,20},{5,21},{6,22},{7,23},{8,24},{9,... | collective-permute-start | bytes 3538952 | tf_op jit(solution)/shard_map/ppermute | solution.py:12
  91.2 240.2 %collective-permute-start.5 = (bf16[1,384,1536]{1,2,0:T(8,128)(2,1)}, bf16[1,384,1536]{1,2,0:T(8,128)(2,1)S(1)}, u32[]{:S(2)}, u32[]{:S(2)}) collective-permute-start(bf16[1,384,1536]{1,2,0:T(8,128)(2,1)} %maximum_bitcast_fusion), channel_id=1, source_target_pairs={{0,15},{1,16},{2,17},{3,18},{4,19},{5,20},{6,21},{7,22},{8,23},{9,... | collective-permute-start | bytes 3538952 | tf_op jit(solution)/shard_map/ppermute | solution.py:12
  114.0 219.1 %collective-permute-start.6 = (bf16[1,384,1536]{1,2,0:T(8,128)(2,1)}, bf16[1,384,1536]{1,2,0:T(8,128)(2,1)S(1)}, u32[]{:S(2)}, u32[]{:S(2)}) collective-permute-start(bf16[1,384,1536]{1,2,0:T(8,128)(2,1)} %maximum_bitcast_fusion), channel_id=1, source_target_pairs={{0,13},{1,14},{2,15},{3,16},{4,17},{5,18},{6,19},{7,20},{8,21},{9,... | collective-permute-start | bytes 3538952 | tf_op jit(solution)/shard_map/ppermute | solution.py:12
  163.8 170.9 %collective-permute-start.7 = (bf16[1,384,1536]{1,2,0:T(8,128)(2,1)}, bf16[1,384,1536]{1,2,0:T(8,128)(2,1)S(1)}, u32[]{:S(2)}, u32[]{:S(2)}) collective-permute-start(bf16[1,384,1536]{1,2,0:T(8,128)(2,1)} %maximum_bitcast_fusion), channel_id=1, source_target_pairs={{0,12},{1,13},{2,14},{3,15},{4,16},{5,17},{6,18},{7,19},{8,20},{9,... | collective-permute-start | bytes 3538952 | tf_op jit(solution)/shard_map/ppermute | solution.py:12
  189.7 148.6 %collective-permute-start.8 = (bf16[1,384,1536]{1,2,0:T(8,128)(2,1)}, bf16[1,384,1536]{1,2,0:T(8,128)(2,1)S(1)}, u32[]{:S(2)}, u32[]{:S(2)}) collective-permute-start(bf16[1,384,1536]{1,2,0:T(8,128)(2,1)} %maximum_bitcast_fusion), channel_id=1, source_target_pairs={{0,11},{1,12},{2,13},{3,14},{4,15},{5,16},{6,17},{7,18},{8,19},{9,... | collective-permute-start | bytes 3538952 | tf_op jit(solution)/shard_map/ppermute | solution.py:12
  228.2 144.1 %collective-permute-start.9 = (bf16[1,384,1536]{1,2,0:T(8,128)(2,1)}, bf16[1,384,1536]{1,2,0:T(8,128)(2,1)S(1)}, u32[]{:S(2)}, u32[]{:S(2)}) collective-permute-start(bf16[1,384,1536]{1,2,0:T(8,128)(2,1)} %maximum_bitcast_fusion), channel_id=1, source_target_pairs={{0,5},{1,6},{2,7},{3,8},{4,9},{5,10},{6,11},{7,12},{8,13},{9,14},{... | collective-permute-start | bytes 3538952 | tf_op jit(solution)/shard_map/ppermute | solution.py:12
  331.5 42.4 %collective-permute-start.10 = (bf16[1,384,1536]{1,2,0:T(8,128)(2,1)}, bf16[1,384,1536]{1,2,0:T(8,128)(2,1)S(1)}, u32[]{:S(2)}, u32[]{:S(2)}) collective-permute-start(bf16[1,384,1536]{1,2,0:T(8,128)(2,1)} %maximum_bitcast_fusion), channel_id=1, source_target_pairs={{0,4},{1,5},{2,6},{3,7},{4,8},{5,9},{6,10},{7,11},{8,12},{9,13},{1... | collective-permute-start | bytes 3538952 | tf_op jit(solution)/shard_map/ppermute | solution.py:12
  333.1 42.5 %collective-permute-start.11 = (bf16[1,384,1536]{1,2,0:T(8,128)(2,1)}, bf16[1,384,1536]{1,2,0:T(8,128)(2,1)S(1)}, u32[]{:S(2)}, u32[]{:S(2)}) collective-permute-start(bf16[1,384,1536]{1,2,0:T(8,128)(2,1)} %maximum_bitcast_fusion), channel_id=1, source_target_pairs={{0,3},{1,4},{2,5},{3,6},{4,7},{5,8},{6,9},{7,10},{8,11},{9,12},{10... | collective-permute-start | bytes 3538952 | tf_op jit(solution)/shard_map/ppermute | solution.py:12
  334.7 53.5 %collective-permute-start.12 = (bf16[1,384,1536]{1,2,0:T(8,128)(2,1)}, bf16[1,384,1536]{1,2,0:T(8,128)(2,1)S(1)}, u32[]{:S(2)}, u32[]{:S(2)}) collective-permute-start(bf16[1,384,1536]{1,2,0:T(8,128)(2,1)} %maximum_bitcast_fusion), channel_id=1, source_target_pairs={{0,1},{1,2},{2,3},{3,4},{4,5},{5,6},{6,7},{7,8},{8,9},{9,10},{10,1... | collective-permute-start | bytes 3538952 | tf_op jit(solution)/shard_map/ppermute | solution.py:12
  338.3 55.7 %collective-permute-start.13 = (bf16[1,384,1536]{1,2,0:T(8,128)(2,1)}, bf16[1,384,1536]{1,2,0:T(8,128)(2,1)S(1)}, u32[]{:S(2)}, u32[]{:S(2)}) collective-permute-start(bf16[1,384,1536]{1,2,0:T(8,128)(2,1)} %maximum_bitcast_fusion), channel_id=1, source_target_pairs={{1,0},{2,1},{3,2},{4,3},{5,4},{6,5},{7,6},{8,7},{9,8},{10,9},{11,1... | collective-permute-start | bytes 3538952 | tf_op jit(solution)/shard_map/ppermute | solution.py:12
  372.3 61.8 %collective-permute-start.14 = (bf16[1,384,1536]{1,2,0:T(8,128)(2,1)}, bf16[1,384,1536]{1,2,0:T(8,128)(2,1)S(1)}, u32[]{:S(2)}, u32[]{:S(2)}) collective-permute-start(bf16[1,384,1536]{1,2,0:T(8,128)(2,1)} %maximum_bitcast_fusion), channel_id=1, source_target_pairs={{3,0},{4,1},{5,2},{6,3},{7,4},{8,5},{9,6},{10,7},{11,8},{12,9},{13... | collective-permute-start | bytes 3538952 | tf_op jit(solution)/shard_map/ppermute | solution.py:12
  373.9 62.0 %collective-permute-start.15 = (bf16[1,384,1536]{1,2,0:T(8,128)(2,1)}, bf16[1,384,1536]{1,2,0:T(8,128)(2,1)S(1)}, u32[]{:S(2)}, u32[]{:S(2)}) collective-permute-start(bf16[1,384,1536]{1,2,0:T(8,128)(2,1)} %maximum_bitcast_fusion), channel_id=1, source_target_pairs={{4,0},{5,1},{6,2},{7,3},{8,4},{9,5},{10,6},{11,7},{12,8},{13,9},{1... | collective-permute-start | bytes 3538952 | tf_op jit(solution)/shard_map/ppermute | solution.py:12
  375.5 96.8 %collective-permute-start.16 = (bf16[1,384,1536]{1,2,0:T(8,128)(2,1)}, bf16[1,384,1536]{1,2,0:T(8,128)(2,1)S(1)}, u32[]{:S(2)}, u32[]{:S(2)}) collective-permute-start(bf16[1,384,1536]{1,2,0:T(8,128)(2,1)} %maximum_bitcast_fusion), channel_id=1, source_target_pairs={{5,0},{6,1},{7,2},{8,3},{9,4},{10,5},{11,6},{12,7},{13,8},{14,9},{... | collective-permute-start | bytes 3538952 | tf_op jit(solution)/shard_map/ppermute | solution.py:12
  388.2 95.1 %collective-permute-start.17 = (bf16[1,384,1536]{1,2,0:T(8,128)(2,1)}, bf16[1,384,1536]{1,2,0:T(8,128)(2,1)S(1)}, u32[]{:S(2)}, u32[]{:S(2)}) collective-permute-start(bf16[1,384,1536]{1,2,0:T(8,128)(2,1)} %maximum_bitcast_fusion), channel_id=1, source_target_pairs={{11,0},{12,1},{13,2},{14,3},{15,4},{16,5},{17,6},{18,7},{19,8},{20... | collective-permute-start | bytes 3538952 | tf_op jit(solution)/shard_map/ppermute | solution.py:12
  394.0 102.2 %collective-permute-start.18 = (bf16[1,384,1536]{1,2,0:T(8,128)(2,1)}, bf16[1,384,1536]{1,2,0:T(8,128)(2,1)S(1)}, u32[]{:S(2)}, u32[]{:S(2)}) collective-permute-start(bf16[1,384,1536]{1,2,0:T(8,128)(2,1)} %maximum_bitcast_fusion), channel_id=1, source_target_pairs={{12,0},{13,1},{14,2},{15,3},{16,4},{17,5},{18,6},{19,7},{20,8},{21... | collective-permute-start | bytes 3538952 | tf_op jit(solution)/shard_map/ppermute | solution.py:12
  434.2 107.9 %collective-permute-start.19 = (bf16[1,384,1536]{1,2,0:T(8,128)(2,1)}, bf16[1,384,1536]{1,2,0:T(8,128)(2,1)S(1)}, u32[]{:S(2)}, u32[]{:S(2)}) collective-permute-start(bf16[1,384,1536]{1,2,0:T(8,128)(2,1)} %maximum_bitcast_fusion), channel_id=1, source_target_pairs={{13,0},{14,1},{15,2},{16,3},{17,4},{18,5},{19,6},{20,7},{21,8},{22... | collective-permute-start | bytes 3538952 | tf_op jit(solution)/shard_map/ppermute | solution.py:12
  435.9 107.7 %collective-permute-start.20 = (bf16[1,384,1536]{1,2,0:T(8,128)(2,1)}, bf16[1,384,1536]{1,2,0:T(8,128)(2,1)S(1)}, u32[]{:S(2)}, u32[]{:S(2)}) collective-permute-start(bf16[1,384,1536]{1,2,0:T(8,128)(2,1)} %maximum_bitcast_fusion), channel_id=1, source_target_pairs={{15,0},{16,1},{17,2},{18,3},{19,4},{20,5},{21,6},{22,7},{23,8},{24... | collective-permute-start | bytes 3538952 | tf_op jit(solution)/shard_map/ppermute | solution.py:12
  472.3 72.8 %collective-permute-start.21 = (bf16[1,384,1536]{1,2,0:T(8,128)(2,1)}, bf16[1,384,1536]{1,2,0:T(8,128)(2,1)S(1)}, u32[]{:S(2)}, u32[]{:S(2)}) collective-permute-start(bf16[1,384,1536]{1,2,0:T(8,128)(2,1)} %maximum_bitcast_fusion), channel_id=1, source_target_pairs={{16,0},{17,1},{18,2},{19,3},{20,4},{21,5},{22,6},{23,7},{24,8},{25... | collective-permute-start | bytes 3538952 | tf_op jit(solution)/shard_map/ppermute | solution.py:12
  483.3 70.5 %collective-permute-start.22 = (bf16[1,384,1536]{1,2,0:T(8,128)(2,1)}, bf16[1,384,1536]{1,2,0:T(8,128)(2,1)S(1)}, u32[]{:S(2)}, u32[]{:S(2)}) collective-permute-start(bf16[1,384,1536]{1,2,0:T(8,128)(2,1)} %maximum_bitcast_fusion), channel_id=1, source_target_pairs={{17,0},{18,1},{19,2},{20,3},{21,4},{22,5},{23,6},{24,7},{25,8},{26... | collective-permute-start | bytes 3538952 | tf_op jit(solution)/shard_map/ppermute | solution.py:12
  496.2 129.3 %collective-permute-start.23 = (bf16[1,384,1536]{1,2,0:T(8,128)(2,1)}, bf16[1,384,1536]{1,2,0:T(8,128)(2,1)S(1)}, u32[]{:S(2)}, u32[]{:S(2)}) collective-permute-start(bf16[1,384,1536]{1,2,0:T(8,128)(2,1)} %maximum_bitcast_fusion), channel_id=1, source_target_pairs={{19,0},{20,1},{21,2},{22,3},{23,4},{24,5},{25,6},{26,7},{27,8},{28... | collective-permute-start | bytes 3538952 | tf_op jit(solution)/shard_map/ppermute | solution.py:12
  542.0 83.7 %collective-permute-start.24 = (bf16[1,384,1536]{1,2,0:T(8,128)(2,1)}, bf16[1,384,1536]{1,2,0:T(8,128)(2,1)S(1)}, u32[]{:S(2)}, u32[]{:S(2)}) collective-permute-start(bf16[1,384,1536]{1,2,0:T(8,128)(2,1)} %maximum_bitcast_fusion), channel_id=1, source_target_pairs={{20,0},{21,1},{22,2},{23,3},{24,4},{25,5},{26,6},{27,7},{28,8},{29... | collective-permute-start | bytes 3538952 | tf_op jit(solution)/shard_map/ppermute | solution.py:12
  543.6 121.5 %collective-permute-start.25 = (bf16[1,384,1536]{1,2,0:T(8,128)(2,1)}, bf16[1,384,1536]{1,2,0:T(8,128)(2,1)S(1)}, u32[]{:S(2)}, u32[]{:S(2)}) collective-permute-start(bf16[1,384,1536]{1,2,0:T(8,128)(2,1)} %maximum_bitcast_fusion), channel_id=1, source_target_pairs={{21,0},{22,1},{23,2},{24,3},{25,4},{26,5},{27,6},{28,7},{29,8},{30... | collective-permute-start | bytes 3538952 | tf_op jit(solution)/shard_map/ppermute | solution.py:12
  665.4 10.8 %copy-start.3 = (bf16[6,384,128]{1,2,0:T(8,128)(2,1)S(1)}, bf16[6,384,128]{1,2,0:T(8,128)(2,1)}, u32[]{:S(2)}) copy-start(bf16[6,384,128]{1,2,0:T(8,128)(2,1)} %custom-call.1) | copy-start | bytes 1769476
  869.7 139.5 %copy-start.4 = (f32[3072]{0:T(1024)S(1)}, f32[3072]{0:T(1024)}, u32[]{:S(2)}) copy-start(f32[3072]{0:T(1024)} %param.18) | copy-start | bytes 36868
  869.7 142.0 %copy-start.1 = (f32[128]{0:T(128)S(1)}, f32[128]{0:T(128)}, u32[]{:S(2)}) copy-start(f32[128]{0:T(128)} %param.15) | copy-start | bytes 1540
Sparse Core Ops, SparseCore 0:
  875.7 133.4 reduce-scatter.1
